TPU v7x, 256 devices: a whole 4x4x8 slice. The times are simulated.
256 devices in a mesh: tm: 64 (over x, y, z_lo), space: 4 (over z_hi, core).
Axes of the slice: x: 4, y: 4, z: 8 (z_hi: 2, z_lo: 4; z = z_hi * 4 + z_lo), core: 2. Of those that a mesh axis runs over, the one named last changes fastest.
Arguments:
- latents: bfloat16 [1, 128, 16, 32, 256], P(None, 'tm', 'space'), may hold values from -24 to 24
- gain_one: float32 [256], replicated, may hold values from 0.25 to 1.75
- conv_one: bfloat16 [3, 3, 3, 256, 256], replicated, may hold values from -0.078125 to 0.078125
- gain_two: float32 [256], replicated, may hold values from 0.25 to 1.75
- conv_two: bfloat16 [3, 3, 3, 256, 256], replicated, may hold values from -0.078125 to 0.078125
- upsample: bfloat16 [3, 256, 256], replicated, may hold values from -0.375 to 0.375
Outputs:
- frames_out: bfloat16 [1, 256, 16, 32, 256], P(None, 'tm', 'space')
All inputs are finite; a program needn't handle non-finite values.
Results may differ from a plain program's by a relative error of at most 0.008.
Values may be sent and summed in bfloat16 or wider, within the bound.
No kernel may reach another device: no remote copies, remote signals or barrier semaphores. Data moves between devices by JAX's collectives and lax.ppermute only.
A program may use at most 64 MiB of HBM per device.

v0:
```python
import jax
import jax.numpy as jnp
from jax import lax
from jax.sharding import PartitionSpec as P


def passed_along(value, axis, by):
    devices = lax.axis_size(axis)
    pairs = [(i, i + by) for i in range(devices) if 0 <= i + by < devices]
    return lax.ppermute(value, axis, pairs)


def with_halo(cells, sides, width):
    for axis, dim in sides:
        count = lax.axis_size(axis)
        ends = count - 1
        head = lax.slice_in_dim(cells, 0, width, axis=dim)
        tail = lax.slice_in_dim(cells, cells.shape[dim] - width, cells.shape[dim], axis=dim)
        cells = jnp.concatenate(
            [
                lax.ppermute(tail, axis, [(i, (i + 1) % count) for i in range(ends)]),
                cells,
                lax.ppermute(head, axis, [((i + 1) % count, i) for i in range(ends)]),
            ],
            axis=dim,
        )
    return cells


def normed_silu(features, gain_vec):
    values = features.astype(jnp.float32)
    mean_square = jnp.mean(values * values, axis=-1, keepdims=True)
    return jax.nn.silu(values * lax.rsqrt(mean_square + 1e-06) * gain_vec).astype(jnp.bfloat16)


def spatial_conv(rimmed, weight):
    widened = jnp.pad(rimmed, ((0, 0), (0, 0), (0, 0), (1, 1), (0, 0)))
    return lax.conv_general_dilated(
        widened,
        weight,
        (1, 1, 1),
        "VALID",
        dimension_numbers=("NDHWC", "DHWIO", "NDHWC"),
        preferred_element_type=jnp.float32,
    )


def with_rims(activation):
    earlier = passed_along(activation[:, -2:], "tm", 1)
    joined = jnp.concatenate([earlier, activation], axis=1)
    return with_halo(joined, (("space", 2),), 1)


def local(latents, gain_one, conv_one, gain_two, conv_two, upsample):
    first_input = normed_silu(latents, gain_one)
    hidden = spatial_conv(with_rims(first_input), conv_one).astype(jnp.bfloat16)
    second_input = normed_silu(hidden, gain_two)
    block_out = (
        latents.astype(jnp.float32) + spatial_conv(with_rims(second_input), conv_two)
    ).astype(jnp.bfloat16)
    earlier_out = passed_along(block_out[:, -1:], "tm", 1)
    previous = jnp.concatenate([earlier_out, block_out[:, :-1]], axis=1)
    channels = block_out.shape[-1]
    flat_rows = block_out.reshape(-1, channels)
    flat_previous = previous.reshape(-1, channels)
    even_frames = jnp.dot(flat_rows, upsample[0], preferred_element_type=jnp.float32)
    even_frames = even_frames + jnp.dot(
        flat_previous, upsample[1], preferred_element_type=jnp.float32
    )
    odd_frames = jnp.dot(flat_rows, upsample[2], preferred_element_type=jnp.float32)
    joined = jnp.stack(
        [even_frames.reshape(block_out.shape), odd_frames.reshape(block_out.shape)], axis=2
    )
    videos, frame_count = (block_out.shape[0], block_out.shape[1])
    return joined.reshape((videos, 2 * frame_count) + block_out.shape[2:]).astype(jnp.bfloat16)


def solution(mesh):
    return jax.shard_map(
        local,
        mesh=mesh,
        in_specs=(P(None, "tm", "space", None, None), P(), P(), P(), P(), P()),
        out_specs=P(None, "tm", "space", None, None),
        check_vma=False,
    )
```

profile of v0, /device:TPU:3, one launch (start us, length us, event | category | flops | bytes accessed | tf_op | source)
XLA Modules:
  0.0 77.6 jit_solution(8352769999748869026)
XLA Ops:
  0.0 1.2 %fusion.20 = f32[2,4,32]{1,2,0:T(8,128)S(1)} fusion(bf16[1,2,4,32,256]{4,3,2,1,0:T(8,128)(2,1)} %param.6), kind=kLoop, calls=%fused_computation.30 | loop fusion | flops 196352 | bytes 132096 | tf_op jit(solution)/shard_map/reduce_sum | solution.py:32
  1.3 1.2 %fusion.25 = bf16[1,2,4,32,256]{4,2,3,1,0:T(4,128)(2,1)S(1)} fusion(f32[256]{0:T(256)} %param.7, f32[2,4,32]{1,2,0:T(8,128)S(1)} %add_rsqrt_fusion.1, bf16[1,2,4,32,256]{4,3,2,1,0:T(8,128)(2,1)} %param.6), kind=kLoop, calls=%fused_computation.35 | loop fusion | flops 524288 | bytes 264192 | tf_op jit(solution)/shard_map/convert_element_type | solution.py:33
  2.4 3.5 %collective-permute-start = (bf16[1,2,4,32,256]{4,2,3,1,0:T(4,128)(2,1)S(1)}, bf16[1,2,4,32,256]{4,2,3,1,0:T(4,128)(2,1)S(1)}, u32[]{:S(2)}, u32[]{:S(2)}) collective-permute-start(bf16[1,2,4,32,256]{4,2,3,1,0:T(4,128)(2,1)S(1)} %fusion.25), channel_id=1, source_target_pairs={{0,4},{4,8},{8,12},{12,16},{16,20},{20,24},{24,28},{28,32},{32,36}... | collective-permute-start | bytes 393224 | tf_op jit(solution)/shard_map/ppermute | solution.py:10
  6.0 8.3 %collective-permute-done = bf16[1,2,4,32,256]{4,2,3,1,0:T(4,128)(2,1)S(1)} collective-permute-done((bf16[1,2,4,32,256]{4,2,3,1,0:T(4,128)(2,1)S(1)}, bf16[1,2,4,32,256]{4,2,3,1,0:T(4,128)(2,1)S(1)}, u32[]{:S(2)}, u32[]{:S(2)}) %collective-permute-start) | collective-permute-done | bytes 131104 | tf_op jit(solution)/shard_map/ppermute | solution.py:10
  14.3 0.2 fusion.31
  14.5 9.4 %collective-permute-start.1 = (bf16[1,4,1,32,256]{4,2,3,1,0:T(2,128)(2,1)S(1)}, bf16[1,4,1,32,256]{4,2,3,1,0:T(2,128)(2,1)S(1)}, u32[]{:S(2)}, u32[]{:S(2)}) collective-permute-start(bf16[1,4,1,32,256]{4,2,3,1,0:T(2,128)(2,1)S(1)} %get-tuple-element.7), channel_id=1, source_target_pairs={{0,1},{1,2},{2,3},{4,5},{5,6},{6,7},{8,9},{9,10},{10,11},{12,13},{... | collective-permute-start | bytes 196616 | tf_op jit(solution)/shard_map/ppermute | solution.py:21
  24.0 1.9 %collective-permute-start.2 = (bf16[1,4,1,32,256]{4,2,3,1,0:T(2,128)(2,1)S(1)}, bf16[1,4,1,32,256]{4,2,3,1,0:T(2,128)(2,1)S(1)}, u32[]{:S(2)}, u32[]{:S(2)}) collective-permute-start(bf16[1,4,1,32,256]{4,2,3,1,0:T(2,128)(2,1)S(1)} %get-tuple-element.8), channel_id=1, source_target_pairs={{1,0},{2,1},{3,2},{5,4},{6,5},{7,6},{9,8},{10,9},{11,10},{13,12},{... | collective-permute-start | bytes 196616 | tf_op jit(solution)/shard_map/ppermute | solution.py:23
  25.9 9.2 %collective-permute-done.2 = bf16[1,4,1,32,256]{4,2,3,1,0:T(2,128)(2,1)S(1)} collective-permute-done((bf16[1,4,1,32,256]{4,2,3,1,0:T(2,128)(2,1)S(1)}, bf16[1,4,1,32,256]{4,2,3,1,0:T(2,128)(2,1)S(1)}, u32[]{:S(2)}, u32[]{:S(2)}) %collective-permute-start.2) | collective-permute-done | bytes 65568 | tf_op jit(solution)/shard_map/ppermute | solution.py:23
  35.2 0.4 maximum_bitcast_fusion
  35.6 0.3 copy.34
  36.3 1.3 %fusion.47 = (f32[2,4,8,5,256]{4,2,3,1,0:T(8,128)S(1)}, f32[2,4,8,5,256]{4,2,3,1,0:T(8,128)S(1)}) fusion(bf16[3,3,3,256,256]{4,3,2,1,0:T(8,128)(2,1)S(1)} %copy-done, bf16[4,6,1,7,2,256]{5,3,4,1,0,2:T(8,128)(2,1)S(1)} %slice.43, bf16[4,6,1,8,5,256]{5,3,4,1,0,2:T(8,128)(2,1)S(1)} %copy.22, pred[8,5]{0,1:T(8,128)(4,1)S(1)} %copy-done.5), kind=kOutput, calls=%fused_computation.70 | convolution fusion | flops 1134854144 | bytes 4857896 | tf_op jit(solution)/shard_map/conv_general_dilated | solution.py:38
  38.1 0.2 copy-done.3
  38.5 1.9 %collective-permute-start.3 = (bf16[1,2,4,32,256]{4,2,3,1,0:T(4,128)(2,1)S(1)}, bf16[1,2,4,32,256]{4,2,3,1,0:T(4,128)(2,1)S(1)}, u32[]{:S(2)}, u32[]{:S(2)}) collective-permute-start(bf16[1,2,4,32,256]{4,2,3,1,0:T(4,128)(2,1)S(1)} %fusion.29), channel_id=1, source_target_pairs={{0,4},{4,8},{8,12},{12,16},{16,20},{20,24},{24,28},{28,32},{32,36}... | collective-permute-start | bytes 393224 | tf_op jit(solution)/shard_map/ppermute | solution.py:10
  40.4 8.7 %collective-permute-done.3 = bf16[1,2,4,32,256]{4,2,3,1,0:T(4,128)(2,1)S(1)} collective-permute-done((bf16[1,2,4,32,256]{4,2,3,1,0:T(4,128)(2,1)S(1)}, bf16[1,2,4,32,256]{4,2,3,1,0:T(4,128)(2,1)S(1)}, u32[]{:S(2)}, u32[]{:S(2)}) %collective-permute-start.3) | collective-permute-done | bytes 131104 | tf_op jit(solution)/shard_map/ppermute | solution.py:10
  49.3 2.8 %collective-permute-start.4 = (bf16[1,4,1,32,256]{4,2,3,1,0:T(2,128)(2,1)S(1)}, bf16[1,4,1,32,256]{4,2,3,1,0:T(2,128)(2,1)S(1)}, u32[]{:S(2)}, u32[]{:S(2)}) collective-permute-start(bf16[1,4,1,32,256]{4,2,3,1,0:T(2,128)(2,1)S(1)} %get-tuple-element.5), channel_id=1, source_target_pairs={{0,1},{1,2},{2,3},{4,5},{5,6},{6,7},{8,9},{9,10},{10,11},{12,13},{... | collective-permute-start | bytes 196616 | tf_op jit(solution)/shard_map/ppermute | solution.py:21
  52.1 1.9 %collective-permute-start.5 = (bf16[1,4,1,32,256]{4,2,3,1,0:T(2,128)(2,1)S(1)}, bf16[1,4,1,32,256]{4,2,3,1,0:T(2,128)(2,1)S(1)}, u32[]{:S(2)}, u32[]{:S(2)}) collective-permute-start(bf16[1,4,1,32,256]{4,2,3,1,0:T(2,128)(2,1)S(1)} %get-tuple-element.6), channel_id=1, source_target_pairs={{1,0},{2,1},{3,2},{5,4},{6,5},{7,6},{9,8},{10,9},{11,10},{13,12},{... | collective-permute-start | bytes 196616 | tf_op jit(solution)/shard_map/ppermute | solution.py:23
  54.1 8.9 %collective-permute-done.5 = bf16[1,4,1,32,256]{4,2,3,1,0:T(2,128)(2,1)S(1)} collective-permute-done((bf16[1,4,1,32,256]{4,2,3,1,0:T(2,128)(2,1)S(1)}, bf16[1,4,1,32,256]{4,2,3,1,0:T(2,128)(2,1)S(1)}, u32[]{:S(2)}, u32[]{:S(2)}) %collective-permute-start.5) | collective-permute-done | bytes 65568 | tf_op jit(solution)/shard_map/ppermute | solution.py:23
  62.9 0.4 maximum_bitcast_fusion.1
  63.4 0.3 copy.35
  64.0 0.9 %copy-done.4 = bf16[3,3,3,256,256]{4,3,2,1,0:T(8,128)(2,1)S(1)} copy-done((bf16[3,3,3,256,256]{4,3,2,1,0:T(8,128)(2,1)S(1)}, bf16[3,3,3,256,256]{4,3,2,1,0:T(8,128)(2,1)}, u32[]{:S(2)}) %copy-start.4) | copy-done | bytes 3538968
  64.9 1.3 %convolution_select_fusion = f32[2,4,8,5,256]{4,2,3,1,0:T(8,128)S(1)} fusion(bf16[3,3,3,256,256]{4,3,2,1,0:T(8,128)(2,1)S(1)} %copy-done.4, bf16[4,6,1,7,2,256]{5,3,4,1,0,2:T(8,128)(2,1)S(1)} %slice.48, bf16[4,6,1,8,5,256]{5,3,4,1,0,2:T(8,128)(2,1)S(1)} %copy.27, pred[8,5]{0,1:T(8,128)(4,1)S(1)} %copy-done.5), kind=kOutput, calls=%fused_computation.4 | convolution fusion | flops 1134608384 | bytes 4530216 | tf_op jit(solution)/shard_map/conv_general_dilated | solution.py:38
  66.7 1.9 %collective-permute-start.6 = (bf16[1,1,4,32,256]{4,2,3,1,0:T(4,128)(2,1)S(1)}, bf16[1,1,4,32,256]{4,2,3,1,0:T(4,128)(2,1)S(1)}, u32[]{:S(2)}, u32[]{:S(2)}) collective-permute-start(bf16[1,1,4,32,256]{4,2,3,1,0:T(4,128)(2,1)S(1)} %get-tuple-element.9), channel_id=1, source_target_pairs={{0,4},{4,8},{8,12},{12,16},{16,20},{20,24},{24,28},{28,32},{32,36}... | collective-permute-start | bytes 196616 | tf_op jit(solution)/shard_map/ppermute | solution.py:10
  69.0 7.5 %collective-permute-done.6 = bf16[1,1,4,32,256]{4,2,3,1,0:T(4,128)(2,1)S(1)} collective-permute-done((bf16[1,1,4,32,256]{4,2,3,1,0:T(4,128)(2,1)S(1)}, bf16[1,1,4,32,256]{4,2,3,1,0:T(4,128)(2,1)S(1)}, u32[]{:S(2)}, u32[]{:S(2)}) %collective-permute-start.6) | collective-permute-done | bytes 65568 | tf_op jit(solution)/shard_map/ppermute | solution.py:10
  76.8 0.7 copy.32
  (35 shorter events, 2.5 us)
Async XLA Ops:
  0.0 36.2 %copy-start = (bf16[3,3,3,256,256]{4,3,2,1,0:T(8,128)(2,1)S(1)}, bf16[3,3,3,256,256]{4,3,2,1,0:T(8,128)(2,1)}, u32[]{:S(2)}) copy-start(bf16[3,3,3,256,256]{4,3,2,1,0:T(8,128)(2,1)} %param.8) | copy-start | bytes 10616836
  2.4 11.9 %collective-permute-start = (bf16[1,2,4,32,256]{4,2,3,1,0:T(4,128)(2,1)S(1)}, bf16[1,2,4,32,256]{4,2,3,1,0:T(4,128)(2,1)S(1)}, u32[]{:S(2)}, u32[]{:S(2)}) collective-permute-start(bf16[1,2,4,32,256]{4,2,3,1,0:T(4,128)(2,1)S(1)} %fusion.25), channel_id=1, source_target_pairs={{0,4},{4,8},{8,12},{12,16},{16,20},{20,24},{24,28},{28,32},{32,36}... | collective-permute-start | bytes 393224 | tf_op jit(solution)/shard_map/ppermute | solution.py:10
  14.5 11.4 %collective-permute-start.1 = (bf16[1,4,1,32,256]{4,2,3,1,0:T(2,128)(2,1)S(1)}, bf16[1,4,1,32,256]{4,2,3,1,0:T(2,128)(2,1)S(1)}, u32[]{:S(2)}, u32[]{:S(2)}) collective-permute-start(bf16[1,4,1,32,256]{4,2,3,1,0:T(2,128)(2,1)S(1)} %get-tuple-element.7), channel_id=1, source_target_pairs={{0,1},{1,2},{2,3},{4,5},{5,6},{6,7},{8,9},{9,10},{10,11},{12,13},{... | collective-permute-start | bytes 196616 | tf_op jit(solution)/shard_map/ppermute | solution.py:21
  24.0 11.2 %collective-permute-start.2 = (bf16[1,4,1,32,256]{4,2,3,1,0:T(2,128)(2,1)S(1)}, bf16[1,4,1,32,256]{4,2,3,1,0:T(2,128)(2,1)S(1)}, u32[]{:S(2)}, u32[]{:S(2)}) collective-permute-start(bf16[1,4,1,32,256]{4,2,3,1,0:T(2,128)(2,1)S(1)} %get-tuple-element.8), channel_id=1, source_target_pairs={{1,0},{2,1},{3,2},{5,4},{6,5},{7,6},{9,8},{10,9},{11,10},{13,12},{... | collective-permute-start | bytes 196616 | tf_op jit(solution)/shard_map/ppermute | solution.py:23
  35.6 0.7 copy-start.5
  37.6 0.7 copy-start.3
  38.5 10.6 %collective-permute-start.3 = (bf16[1,2,4,32,256]{4,2,3,1,0:T(4,128)(2,1)S(1)}, bf16[1,2,4,32,256]{4,2,3,1,0:T(4,128)(2,1)S(1)}, u32[]{:S(2)}, u32[]{:S(2)}) collective-permute-start(bf16[1,2,4,32,256]{4,2,3,1,0:T(4,128)(2,1)S(1)} %fusion.29), channel_id=1, source_target_pairs={{0,4},{4,8},{8,12},{12,16},{16,20},{20,24},{24,28},{28,32},{32,36}... | collective-permute-start | bytes 393224 | tf_op jit(solution)/shard_map/ppermute | solution.py:10
  49.3 4.8 %collective-permute-start.4 = (bf16[1,4,1,32,256]{4,2,3,1,0:T(2,128)(2,1)S(1)}, bf16[1,4,1,32,256]{4,2,3,1,0:T(2,128)(2,1)S(1)}, u32[]{:S(2)}, u32[]{:S(2)}) collective-permute-start(bf16[1,4,1,32,256]{4,2,3,1,0:T(2,128)(2,1)S(1)} %get-tuple-element.5), channel_id=1, source_target_pairs={{0,1},{1,2},{2,3},{4,5},{5,6},{6,7},{8,9},{9,10},{10,11},{12,13},{... | collective-permute-start | bytes 196616 | tf_op jit(solution)/shard_map/ppermute | solution.py:21
  52.1 10.8 %collective-permute-start.5 = (bf16[1,4,1,32,256]{4,2,3,1,0:T(2,128)(2,1)S(1)}, bf16[1,4,1,32,256]{4,2,3,1,0:T(2,128)(2,1)S(1)}, u32[]{:S(2)}, u32[]{:S(2)}) collective-permute-start(bf16[1,4,1,32,256]{4,2,3,1,0:T(2,128)(2,1)S(1)} %get-tuple-element.6), channel_id=1, source_target_pairs={{1,0},{2,1},{3,2},{5,4},{6,5},{7,6},{9,8},{10,9},{11,10},{13,12},{... | collective-permute-start | bytes 196616 | tf_op jit(solution)/shard_map/ppermute | solution.py:23
  62.9 2.0 %copy-start.4 = (bf16[3,3,3,256,256]{4,3,2,1,0:T(8,128)(2,1)S(1)}, bf16[3,3,3,256,256]{4,3,2,1,0:T(8,128)(2,1)}, u32[]{:S(2)}) copy-start(bf16[3,3,3,256,256]{4,3,2,1,0:T(8,128)(2,1)} %param.10) | copy-start | bytes 10616836
  64.9 1.5 %copy-start.1 = (bf16[1,2,4,32,256]{4,3,2,1,0:T(8,128)(2,1)S(1)}, bf16[1,2,4,32,256]{4,3,2,1,0:T(8,128)(2,1)}, u32[]{:S(2)}) copy-start(bf16[1,2,4,32,256]{4,3,2,1,0:T(8,128)(2,1)} %param.6) | copy-start | bytes 393220
  66.3 2.3 %copy-start.2 = (bf16[3,256,256]{2,1,0:T(8,128)(2,1)S(1)}, bf16[3,256,256]{2,1,0:T(8,128)(2,1)}, u32[]{:S(2)}) copy-start(bf16[3,256,256]{2,1,0:T(8,128)(2,1)} %param.11) | copy-start | bytes 1179652
  66.7 9.8 %collective-permute-start.6 = (bf16[1,1,4,32,256]{4,2,3,1,0:T(4,128)(2,1)S(1)}, bf16[1,1,4,32,256]{4,2,3,1,0:T(4,128)(2,1)S(1)}, u32[]{:S(2)}, u32[]{:S(2)}) collective-permute-start(bf16[1,1,4,32,256]{4,2,3,1,0:T(4,128)(2,1)S(1)} %get-tuple-element.9), channel_id=1, source_target_pairs={{0,4},{4,8},{8,12},{12,16},{16,20},{20,24},{24,28},{28,32},{32,36}... | collective-permute-start | bytes 196616 | tf_op jit(solution)/shard_map/ppermute | solution.py:10
where the time goes:
time: 77.9 us; the launch traced here: 77.6 us
  waiting for transfers between devices  42.6 us (55%)
  starting transfers between devices  23.5 us (30%)
  other arithmetic  4.33 us (6%)
  local copies, waits for them, and re-layouts  3.62 us (5%)
  matrix products  3.21 us (4%)
    ppermute x3, waiting for transfers between devices, passed_along(): return lax.ppermute(value, axis, pairs)  24.5 us
    ppermute x2, waiting for transfers between devices, with_halo(): lax.ppermute(head, axis, [((i + 1) % count, i) for i in range(ends)])  18.1 us
    ppermute x2, starting transfers between devices, with_halo(): lax.ppermute(tail, axis, [(i, (i + 1) % count) for i in range(ends)])  12.3 us
    ppermute x3, starting transfers between devices, passed_along(): return lax.ppermute(value, axis, pairs)  7.39 us
    ppermute x2, starting transfers between devices, with_halo(): lax.ppermute(head, axis, [((i + 1) % count, i) for i in range(ends)])  3.84 us
    conv_general_dilated x2, matrix products, spatial_conv(): lax.conv_general_dilated(widened, weight, (1, 1, 1), 'VALID', dimension_n...  2.66 us
    unnamed x14, local copies, waits for them, and re-layouts  1.84 us
  transfers between devices with their start and end apart: 7, of which 5 were waited for; matrix products, arithmetic and copies ran while one was open for 0% of the time, Pallas kernels for 0%

commit v1 on v0

v1 whole, which is shorter than its diff:
```python
import functools

import jax
import jax.numpy as jnp
from jax import lax
from jax.experimental import pallas as pl
from jax.experimental.pallas import tpu as pltpu
from jax.sharding import PartitionSpec as P

AXES = ("tm", "space")


def moved(value, target):
    count, tiles = lax.axis_size("tm"), lax.axis_size("space")
    pairs = []
    for t in range(count):
        for s in range(tiles):
            to = target(t, s)
            if to is not None and 0 <= to[0] < count:
                pairs.append((t * tiles + s, to[0] * tiles + to[1]))
    return lax.ppermute(value, AXES, pairs)


def swapped(value):
    return moved(value, lambda t, s: (t, s ^ 1))


def to_inner(value, by):
    return moved(value, lambda t, s: (t + by, s ^ 1) if s in (0, 3) else None)


def across(value, by):
    return moved(value, lambda t, s: (t + by, s ^ 2) if s in (0, 3) else None)


def to_outer(value):
    return moved(value, lambda t, s: (t, s ^ 1) if s in (1, 2) else None)


def normed_silu(values, gain):
    mean_square = jnp.mean(values * values, axis=-1, keepdims=True)
    scaled = values * lax.rsqrt(mean_square + 1e-06) * gain
    return scaled * jax.nn.sigmoid(scaled)


def put_shifted(buffer, frame, row, activation):
    rows, width, channels = activation.shape
    zero = jnp.zeros((rows, 1, channels), jnp.float32)
    left = jnp.concatenate([zero, activation[:, :-1]], axis=1)
    right = jnp.concatenate([activation[:, 1:], zero], axis=1)
    for i, part in enumerate((left, activation, right)):
        buffer[frame, pl.ds(row, rows), :, i * channels : (i + 1) * channels] = part.astype(jnp.bfloat16)


def conv(buffer, weight, total, frames, rows):
    channels = total.shape[-1]
    width = buffer.shape[2]

    def tap(i, carry):
        dt, di = i // 3, lax.rem(i, 3)
        lhs = buffer[pl.ds(dt, frames), pl.ds(di, rows)].reshape(frames * rows * width, 3 * channels)
        rhs = weight[i]
        part = jnp.dot(lhs, rhs, preferred_element_type=jnp.float32)

        @pl.when(i == 0)
        def _():
            total[...] = part

        @pl.when(i > 0)
        def _():
            total[...] += part

        return carry

    lax.fori_loop(0, 9, tap, 0)


def block_kernel(
    spot, x, m, p1, p2, p3, q1, q2, q3, z0, z1, z2, z3, gain_one, conv_one, gain_two, conv_two, upsample, out, first, total_one, second, total_two
):
    tile, width, channels = x.shape[1], x.shape[2], x.shape[3]
    s = spot[0]
    even = lax.rem(s, 2) == 0
    inner = jnp.logical_or(s == 1, s == 2)
    own_at = jnp.where(inner, tile, 0)
    mate_at = jnp.where(inner, 0, tile) + jnp.where(even, 0, 2)
    mate_to = jnp.where(even, 6, 0)
    other_to = jnp.where(even, 0, 6)
    gain = gain_one[...].reshape(1, 1, channels)

    def put(frame, row, ref, at, src, rows):
        values = ref[src, pl.ds(at, rows)].astype(jnp.float32)
        put_shifted(first, frame, row, normed_silu(values, gain))

    for f in range(2):
        put(5 + f, 2, x, 0, f, tile)
        put(5 + f, mate_to, m, jnp.where(even, 0, 2), f, 2)

    @pl.when(inner)
    def _():
        for frame, ref, src in ((4, p1, 1), (3, p1, 0), (2, p2, 1), (1, p2, 0), (0, p3, 0)):
            put(frame, 2, ref, own_at, src, tile)
            put(frame, mate_to, ref, mate_at, src, 2)
        for frame, ref, src in ((6, z0, 1), (5, z0, 0), (4, z1, 1), (3, z1, 0), (2, z2, 1), (1, z2, 0), (0, z3, 0)):
            put(frame, other_to, ref, 0, src, 2)

    @pl.when(jnp.logical_not(inner))
    def _():
        for frame, ref, src in ((4, q1, 1), (3, q1, 0), (2, q2, 1), (1, q2, 0), (0, q3, 0)):
            put(frame, 2, ref, own_at, src, tile)
            put(frame, mate_to, ref, mate_at, src, 2)
        for frame in range(7):
            first[frame, pl.ds(other_to, 2)] = jnp.zeros((2, width, 3 * channels), jnp.bfloat16)

    conv(first, conv_one, total_one, 5, 6)
    gain_later = gain_two[...].reshape(1, 1, channels)

    def renorm(f, carry):
        at = pl.multiple_of(f * 6 * width, 6 * width)
        hidden = total_one[pl.ds(at, 6 * width)].reshape(6, width, channels)
        hidden = hidden.astype(jnp.bfloat16).astype(jnp.float32)
        put_shifted(second, f, 0, normed_silu(hidden, gain_later))
        return carry

    lax.fori_loop(0, 5, renorm, 0)

    @pl.when(jnp.logical_not(inner))
    def _():
        edge = jnp.where(even, 0, 5)
        for f in range(5):
            second[f, pl.ds(edge, 1)] = jnp.zeros((1, width, 3 * channels), jnp.bfloat16)

    conv(second, conv_two, total_two, 3, 4)
    cells = tile * width
    before = jnp.where(inner, p1[1, pl.ds(own_at, tile)], q1[1, pl.ds(own_at, tile)])
    block = []
    for f, latents in enumerate((before, x[0], x[1])):
        total = total_two[f * cells : (f + 1) * cells] + latents.reshape(cells, channels).astype(jnp.float32)
        block.append(total.astype(jnp.bfloat16))
    now = jnp.concatenate(block[1:], axis=0)
    earlier = jnp.concatenate(block[:-1], axis=0)
    even_frames = jnp.dot(now, upsample[0], preferred_element_type=jnp.float32)
    even_frames = even_frames + jnp.dot(earlier, upsample[1], preferred_element_type=jnp.float32)
    odd_frames = jnp.dot(now, upsample[2], preferred_element_type=jnp.float32)
    for f in range(2):
        part = slice(f * cells, (f + 1) * cells)
        out[2 * f] = even_frames[part].astype(jnp.bfloat16).reshape(tile, width, channels)
        out[2 * f + 1] = odd_frames[part].astype(jnp.bfloat16).reshape(tile, width, channels)


def local(latents, gain_one, conv_one, gain_two, conv_two, upsample):
    x = latents[0]
    frames, tile, width, channels = x.shape
    s = lax.axis_index("space")
    m = swapped(x)
    chip = jnp.concatenate([x, m], axis=1)
    edge = jnp.where(s < 2, m[:, tile - 2 :], m[:, :2])
    z0 = across(edge, 0)
    p1 = to_inner(chip, 1)
    p2 = to_inner(chip, 2)
    p3 = to_inner(chip[1:], 3)
    z3 = across(edge[1:], 3)
    z2 = across(edge, 2)
    z1 = across(edge, 1)
    q1, q2, q3 = to_outer(p1), to_outer(p2), to_outer(p3)
    vmem = pl.BlockSpec(memory_space=pltpu.VMEM)
    out = pl.pallas_call(
        block_kernel,
        out_shape=jax.ShapeDtypeStruct((2 * frames, tile, width, channels), jnp.bfloat16),
        in_specs=[pl.BlockSpec(memory_space=pltpu.SMEM)] + [vmem] * 17,
        out_specs=vmem,
        scratch_shapes=[
            pltpu.VMEM((7, 8, width, 3 * channels), jnp.bfloat16),
            pltpu.VMEM((5 * 6 * width, channels), jnp.float32),
            pltpu.VMEM((5, 6, width, 3 * channels), jnp.bfloat16),
            pltpu.VMEM((3 * 4 * width, channels), jnp.float32),
        ],
        compiler_params=pltpu.CompilerParams(vmem_limit_bytes=48 * 1024 * 1024),
        name="block",
    )(
        s.reshape(1).astype(jnp.int32), x, m, p1, p2, p3, q1, q2, q3, z0, z1, z2, z3,
        gain_one.reshape(1, channels), conv_one.reshape(9, 3 * channels, channels),
        gain_two.reshape(1, channels), conv_two.reshape(9, 3 * channels, channels), upsample,
    )
    return out[None]


def solution(mesh):
    return jax.shard_map(
        local,
        mesh=mesh,
        in_specs=(P(None, "tm", "space", None, None), P(), P(), P(), P(), P()),
        out_specs=P(None, "tm", "space", None, None),
        check_vma=False,
    )
```

time: 77.9 us -> 71.3 us (0.915)
  Pallas kernels: 0 us -> 13.8 us
  waiting for transfers between devices: 42.6 us -> 31.1 us
  starting transfers between devices: 23.5 us -> 18.3 us
  matrix products: 3.21 us -> 0 us
  other arithmetic: 4.33 us -> 1.8 us
  local copies, waits for them, and re-layouts: 3.62 us -> 5.26 us
    pallas_call x0 -> x1, Pallas kernels: none -> 13.8 us  [local(): pl.pallas_call(block_kernel, out_shape=jax.ShapeDtypeStruct((2 * frames,...]
    ppermute x7 -> x11, waiting for transfers between devices: 42.6 us -> 31.1 us  [moved(): return lax.ppermute(value, AXES, pairs)]
    ppermute x7 -> x11, starting transfers between devices: 23.5 us -> 18.3 us  [moved(): return lax.ppermute(value, AXES, pairs)]
    unnamed x14 -> x10, local copies, waits for them, and re-layouts: 1.84 us -> 5.25 us
    conv_general_dilated x2 -> x0, matrix products: 2.66 us -> none  [spatial_conv(): lax.conv_general_dilated(widened, weight, (1, 1, 1), 'VALID', dimension_n...]
    convert_element_type x3 -> x0, other arithmetic: 1.53 us -> none  [the longest x2 1.39 us: normed_silu(): jax.nn.silu(values * lax.rsqrt(mean_square + 1e-06) * gain_vec)]
    reduce_sum x2 -> x0, other arithmetic: 1.37 us -> none  [normed_silu(): mean_square = jnp.mean(values * values, axis=-1, keepdims=True)]
    concatenate x5 -> x2, other arithmetic: 1.37 us -> 1.78 us  [local(): chip = jnp.concatenate([x, m], axis=1)]
  transfers between devices with their start and end apart: 7 -> 11, of which waited for: 5 -> 5; matrix products, arithmetic and copies ran while one was open for 0% -> 1% of each run, Pallas kernels for 0% -> 0%
where the time goes in v1:
time: 71.3 us; the launch traced here: 70.4 us
  waiting for transfers between devices  31.1 us (44%)
  starting transfers between devices  18.3 us (26%)
  Pallas kernels  13.8 us (19%)
  local copies, waits for them, and re-layouts  5.26 us (7%)
  other arithmetic  1.8 us (3%)
    ppermute x11, waiting for transfers between devices, moved(): return lax.ppermute(value, AXES, pairs)  31.1 us
    ppermute x11, starting transfers between devices, moved(): return lax.ppermute(value, AXES, pairs)  18.3 us
    pallas_call x1, Pallas kernels, local(): pl.pallas_call(block_kernel, out_shape=jax.ShapeDtypeStruct((2 * frames,...  13.8 us
    unnamed x10, local copies, waits for them, and re-layouts  5.25 us
    concatenate x2, other arithmetic, local(): chip = jnp.concatenate([x, m], axis=1)  1.78 us
  transfers between devices with their start and end apart: 11, of which 5 were waited for; matrix products, arithmetic and copies ran while one was open for 1% of the time, Pallas kernels for 0%

profile of v1, /device:TPU:3, one launch (start us, length us, event | category | flops | bytes accessed | tf_op | source)
XLA Modules:
  0.0 70.4 jit_solution(17937947599581930664)
XLA Ops:
  0.0 0.7 collective-permute-start
  0.7 1.2 %collective-permute-done.m = bf16[2,4,32,256]{3,2,1,0:T(8,128)(2,1)S(1)} collective-permute-done((bf16[2,4,32,256]{3,2,1,0:T(8,128)(2,1)}, bf16[2,4,32,256]{3,2,1,0:T(8,128)(2,1)S(1)}, u32[]{:S(2)}, u32[]{:S(2)}) %collective-permute-start) | collective-permute-done | bytes 131104 | tf_op jit(solution)/shard_map/ppermute | solution.py:21
  1.9 0.9 %pad_maximum_fusion = bf16[2,8,32,256]{3,2,1,0:T(8,128)(2,1)S(1)} fusion(bf16[2,4,32,256]{3,2,1,0:T(8,128)(2,1)S(1)} %collective-permute-done.m, bf16[2,4,32,256]{3,2,1,0:T(8,128)(2,1)} %bitcast.9), kind=kLoop, calls=%fused_computation.1 | loop fusion | flops 131072 | bytes 524288 | tf_op jit(solution)/shard_map/concatenate | solution.py:156
  2.8 1.3 %collective-permute-start.2 = (bf16[2,8,32,256]{3,2,1,0:T(8,128)(2,1)S(1)}, bf16[2,8,32,256]{3,2,1,0:T(8,128)(2,1)S(1)}, u32[]{:S(2)}, u32[]{:S(2)}) collective-permute-start(bf16[2,8,32,256]{3,2,1,0:T(8,128)(2,1)S(1)} %pad_maximum_fusion), channel_id=1, source_target_pairs={{0,9},{3,10},{4,13},{7,14},{8,17},{11,18},{12,21},{15,22},{16,25},... | collective-permute-start | bytes 786440 | tf_op jit(solution)/shard_map/ppermute | solution.py:21
  4.1 1.3 %collective-permute-start.1 = (bf16[2,8,32,256]{3,2,1,0:T(8,128)(2,1)S(1)}, bf16[2,8,32,256]{3,2,1,0:T(8,128)(2,1)S(1)}, u32[]{:S(2)}, u32[]{:S(2)}) collective-permute-start(bf16[2,8,32,256]{3,2,1,0:T(8,128)(2,1)S(1)} %pad_maximum_fusion), channel_id=1, source_target_pairs={{0,5},{3,6},{4,9},{7,10},{8,13},{11,14},{12,17},{15,18},{16,21},{1... | collective-permute-start | bytes 786440 | tf_op jit(solution)/shard_map/ppermute | solution.py:21
  5.4 0.9 %fusion = bf16[1,8,32,256]{3,2,1,0:T(8,128)(2,1)S(1)} fusion(bf16[2,4,32,256]{3,2,1,0:T(8,128)(2,1)} %bitcast.10, bf16[2,4,32,256]{3,2,1,0:T(8,128)(2,1)S(1)} %collective-permute-done.m), kind=kLoop, calls=%fused_computation.3 | loop fusion | flops 65536 | bytes 393216 | tf_op jit(solution)/shard_map/concatenate | solution.py:156
  6.3 1.3 %collective-permute-start.3 = (bf16[1,8,32,256]{3,2,1,0:T(8,128)(2,1)S(1)}, bf16[1,8,32,256]{3,2,1,0:T(8,128)(2,1)S(1)}, u32[]{:S(2)}, u32[]{:S(2)}) collective-permute-start(bf16[1,8,32,256]{3,2,1,0:T(8,128)(2,1)S(1)} %fusion), channel_id=1, source_target_pairs={{0,13},{3,14},{4,17},{7,18},{8,21},{11,22},{12,25},{15,26},{16,29}... | collective-permute-start | bytes 393224 | tf_op jit(solution)/shard_map/ppermute | solution.py:21
  7.6 12.5 %collective-permute-done.2.p2 = bf16[2,8,32,256]{3,2,1,0:T(8,128)(2,1)S(1)} collective-permute-done((bf16[2,8,32,256]{3,2,1,0:T(8,128)(2,1)S(1)}, bf16[2,8,32,256]{3,2,1,0:T(8,128)(2,1)S(1)}, u32[]{:S(2)}, u32[]{:S(2)}) %collective-permute-start.2) | collective-permute-done | bytes 262176 | tf_op jit(solution)/shard_map/ppermute | solution.py:21
  20.1 1.3 %collective-permute-start.5 = (bf16[2,8,32,256]{3,2,1,0:T(8,128)(2,1)S(1)}, bf16[2,8,32,256]{3,2,1,0:T(8,128)(2,1)S(1)}, u32[]{:S(2)}, u32[]{:S(2)}) collective-permute-start(bf16[2,8,32,256]{3,2,1,0:T(8,128)(2,1)S(1)} %collective-permute-done.2.p2), channel_id=1, source_target_pairs={{1,0},{2,3},{5,4},{6,7},{9,8},{10,11},{13,12},{14,15},{17,16},{18,... | collective-permute-start | bytes 786440 | tf_op jit(solution)/shard_map/ppermute | solution.py:21
  21.4 1.3 %collective-permute-start.4 = (bf16[2,8,32,256]{3,2,1,0:T(8,128)(2,1)S(1)}, bf16[2,8,32,256]{3,2,1,0:T(8,128)(2,1)S(1)}, u32[]{:S(2)}, u32[]{:S(2)}) collective-permute-start(bf16[2,8,32,256]{3,2,1,0:T(8,128)(2,1)S(1)} %collective-permute-done.1.p1), channel_id=1, source_target_pairs={{1,0},{2,3},{5,4},{6,7},{9,8},{10,11},{13,12},{14,15},{17,16},{18,... | collective-permute-start | bytes 786440 | tf_op jit(solution)/shard_map/ppermute | solution.py:21
  22.8 1.3 %collective-permute-start.9 = (bf16[2,2,32,256]{3,2,1,0:T(8,128)(2,1)S(1)}, bf16[2,2,32,256]{3,2,1,0:T(8,128)(2,1)S(1)}, u32[]{:S(2)}, u32[]{:S(2)}) collective-permute-start(bf16[2,2,32,256]{3,2,1,0:T(8,128)(2,1)S(1)} %slice_select_fusion), channel_id=1, source_target_pairs={{0,10},{3,9},{4,14},{7,13},{8,18},{11,17},{12,22},{15,21},{16,26},... | collective-permute-start | bytes 196616 | tf_op jit(solution)/shard_map/ppermute | solution.py:21
  24.1 5.9 %collective-permute-start.6 = (bf16[1,8,32,256]{3,2,1,0:T(8,128)(2,1)S(1)}, bf16[1,8,32,256]{3,2,1,0:T(8,128)(2,1)S(1)}, u32[]{:S(2)}, u32[]{:S(2)}) collective-permute-start(bf16[1,8,32,256]{3,2,1,0:T(8,128)(2,1)S(1)} %collective-permute-done.3.p3), channel_id=1, source_target_pairs={{1,0},{2,3},{5,4},{6,7},{9,8},{10,11},{13,12},{14,15},{17,16},{18,... | collective-permute-start | bytes 393224 | tf_op jit(solution)/shard_map/ppermute | solution.py:21
  30.0 1.3 %collective-permute-start.10 = (bf16[1,2,32,256]{3,2,1,0:T(8,128)(2,1)S(1)}, bf16[1,2,32,256]{3,2,1,0:T(8,128)(2,1)S(1)}, u32[]{:S(2)}, u32[]{:S(2)}) collective-permute-start(bf16[1,2,32,256]{3,2,1,0:T(8,128)(2,1)S(1)} %slice.20), channel_id=1, source_target_pairs={{0,14},{3,13},{4,18},{7,17},{8,22},{11,21},{12,26},{15,25},{16,30}... | collective-permute-start | bytes 98312 | tf_op jit(solution)/shard_map/ppermute | solution.py:21
  31.3 9.7 %collective-permute-done.10.z3 = bf16[1,2,32,256]{3,2,1,0:T(8,128)(2,1)S(1)} collective-permute-done((bf16[1,2,32,256]{3,2,1,0:T(8,128)(2,1)S(1)}, bf16[1,2,32,256]{3,2,1,0:T(8,128)(2,1)S(1)}, u32[]{:S(2)}, u32[]{:S(2)}) %collective-permute-start.10) | collective-permute-done | bytes 32800 | tf_op jit(solution)/shard_map/ppermute | solution.py:21
  41.0 1.3 %collective-permute-start.8 = (bf16[2,2,32,256]{3,2,1,0:T(8,128)(2,1)S(1)}, bf16[2,2,32,256]{3,2,1,0:T(8,128)(2,1)S(1)}, u32[]{:S(2)}, u32[]{:S(2)}) collective-permute-start(bf16[2,2,32,256]{3,2,1,0:T(8,128)(2,1)S(1)} %slice_select_fusion), channel_id=1, source_target_pairs={{0,6},{3,5},{4,10},{7,9},{8,14},{11,13},{12,18},{15,17},{16,22},{1... | collective-permute-start | bytes 196616 | tf_op jit(solution)/shard_map/ppermute | solution.py:21
  42.3 1.3 %collective-permute-start.7 = (bf16[2,2,32,256]{3,2,1,0:T(8,128)(2,1)S(1)}, bf16[2,2,32,256]{3,2,1,0:T(8,128)(2,1)S(1)}, u32[]{:S(2)}, u32[]{:S(2)}) collective-permute-start(bf16[2,2,32,256]{3,2,1,0:T(8,128)(2,1)S(1)} %slice_select_fusion), channel_id=1, source_target_pairs={{0,2},{3,1},{4,6},{7,5},{8,10},{11,9},{12,14},{15,13},{16,18},{19,... | collective-permute-start | bytes 196616 | tf_op jit(solution)/shard_map/ppermute | solution.py:21
  43.6 6.6 %collective-permute-done.8.z1 = bf16[2,2,32,256]{3,2,1,0:T(8,128)(2,1)S(1)} collective-permute-done((bf16[2,2,32,256]{3,2,1,0:T(8,128)(2,1)S(1)}, bf16[2,2,32,256]{3,2,1,0:T(8,128)(2,1)S(1)}, u32[]{:S(2)}, u32[]{:S(2)}) %collective-permute-start.8) | collective-permute-done | bytes 65568 | tf_op jit(solution)/shard_map/ppermute | solution.py:21
  50.3 1.0 %collective-permute-done.7.z0 = bf16[2,2,32,256]{3,2,1,0:T(8,128)(2,1)S(1)} collective-permute-done((bf16[2,2,32,256]{3,2,1,0:T(8,128)(2,1)S(1)}, bf16[2,2,32,256]{3,2,1,0:T(8,128)(2,1)S(1)}, u32[]{:S(2)}, u32[]{:S(2)}) %collective-permute-start.7) | collective-permute-done | bytes 65568 | tf_op jit(solution)/shard_map/ppermute | solution.py:21
  51.3 2.0 %copy-done = bf16[3,3,3,256,256]{4,3,2,1,0:T(8,128)(2,1)S(1)} copy-done((bf16[3,3,3,256,256]{4,3,2,1,0:T(8,128)(2,1)S(1)}, bf16[3,3,3,256,256]{4,3,2,1,0:T(8,128)(2,1)}, u32[]{:S(2)}) %copy-start) | copy-done | bytes 3538968
  53.3 0.9 %copy-done.1 = bf16[1,2,4,32,256]{4,3,2,1,0:T(8,128)(2,1)S(1)} copy-done((bf16[1,2,4,32,256]{4,3,2,1,0:T(8,128)(2,1)S(1)}, bf16[1,2,4,32,256]{4,3,2,1,0:T(8,128)(2,1)}, u32[]{:S(2)}) %copy-start.1) | copy-done | bytes 131096
  54.2 1.0 %copy-done.2 = bf16[3,256,256]{2,1,0:T(8,128)(2,1)S(1)} copy-done((bf16[3,256,256]{2,1,0:T(8,128)(2,1)S(1)}, bf16[3,256,256]{2,1,0:T(8,128)(2,1)}, u32[]{:S(2)}) %copy-start.2) | copy-done | bytes 393240
  55.2 0.7 copy-done.3
  55.9 0.7 copy-done.4
  56.5 13.8 %block.1 = bf16[4,4,32,256]{3,2,1,0:T(8,128)(2,1)} custom-call(s32[1]{0:T(128)} %bitcast.spot, bf16[2,4,32,256]{3,2,1,0:T(8,128)(2,1)S(1)} %bitcast.11, bf16[2,4,32,256]{3,2,1,0:T(8,128)(2,1)S(1)} %collective-permute-done.m, bf16[2,8,32,256]{3,2,1,0:T(8,128)(2,1)S(1)} %collective-permute-done.1.p1, bf16[2,8,32,256]{3,2,1,0:T(8,128)(2,1)S(1)} %collective-permute-done.2.p2, ...), custom_call_target="tpu_custom_call" | custom-call | tf_op jit(solution)/shard_map/block/pallas_call | solution.py:167
  (13 shorter events, 0.0 us)
Async XLA Ops:
  0.0 1.9 %collective-permute-start = (bf16[2,4,32,256]{3,2,1,0:T(8,128)(2,1)}, bf16[2,4,32,256]{3,2,1,0:T(8,128)(2,1)S(1)}, u32[]{:S(2)}, u32[]{:S(2)}) collective-permute-start(bf16[2,4,32,256]{3,2,1,0:T(8,128)(2,1)} %bitcast.8), channel_id=1, source_target_pairs={{0,1},{1,0},{2,3},{3,2},{4,5},{5,4},{6,7},{7,6},{8,9},{9,8},{10,11... | collective-permute-start | bytes 393224 | tf_op jit(solution)/shard_map/ppermute | solution.py:21
  2.8 17.3 %collective-permute-start.2 = (bf16[2,8,32,256]{3,2,1,0:T(8,128)(2,1)S(1)}, bf16[2,8,32,256]{3,2,1,0:T(8,128)(2,1)S(1)}, u32[]{:S(2)}, u32[]{:S(2)}) collective-permute-start(bf16[2,8,32,256]{3,2,1,0:T(8,128)(2,1)S(1)} %pad_maximum_fusion), channel_id=1, source_target_pairs={{0,9},{3,10},{4,13},{7,14},{8,17},{11,18},{12,21},{15,22},{16,25},... | collective-permute-start | bytes 786440 | tf_op jit(solution)/shard_map/ppermute | solution.py:21
  4.1 17.3 %collective-permute-start.1 = (bf16[2,8,32,256]{3,2,1,0:T(8,128)(2,1)S(1)}, bf16[2,8,32,256]{3,2,1,0:T(8,128)(2,1)S(1)}, u32[]{:S(2)}, u32[]{:S(2)}) collective-permute-start(bf16[2,8,32,256]{3,2,1,0:T(8,128)(2,1)S(1)} %pad_maximum_fusion), channel_id=1, source_target_pairs={{0,5},{3,6},{4,9},{7,10},{8,13},{11,14},{12,17},{15,18},{16,21},{1... | collective-permute-start | bytes 786440 | tf_op jit(solution)/shard_map/ppermute | solution.py:21
  6.3 17.8 %collective-permute-start.3 = (bf16[1,8,32,256]{3,2,1,0:T(8,128)(2,1)S(1)}, bf16[1,8,32,256]{3,2,1,0:T(8,128)(2,1)S(1)}, u32[]{:S(2)}, u32[]{:S(2)}) collective-permute-start(bf16[1,8,32,256]{3,2,1,0:T(8,128)(2,1)S(1)} %fusion), channel_id=1, source_target_pairs={{0,13},{3,14},{4,17},{7,18},{8,21},{11,22},{12,25},{15,26},{16,29}... | collective-permute-start | bytes 393224 | tf_op jit(solution)/shard_map/ppermute | solution.py:21
  20.1 31.1 %collective-permute-start.5 = (bf16[2,8,32,256]{3,2,1,0:T(8,128)(2,1)S(1)}, bf16[2,8,32,256]{3,2,1,0:T(8,128)(2,1)S(1)}, u32[]{:S(2)}, u32[]{:S(2)}) collective-permute-start(bf16[2,8,32,256]{3,2,1,0:T(8,128)(2,1)S(1)} %collective-permute-done.2.p2), channel_id=1, source_target_pairs={{1,0},{2,3},{5,4},{6,7},{9,8},{10,11},{13,12},{14,15},{17,16},{18,... | collective-permute-start | bytes 786440 | tf_op jit(solution)/shard_map/ppermute | solution.py:21
  21.4 29.8 %collective-permute-start.4 = (bf16[2,8,32,256]{3,2,1,0:T(8,128)(2,1)S(1)}, bf16[2,8,32,256]{3,2,1,0:T(8,128)(2,1)S(1)}, u32[]{:S(2)}, u32[]{:S(2)}) collective-permute-start(bf16[2,8,32,256]{3,2,1,0:T(8,128)(2,1)S(1)} %collective-permute-done.1.p1), channel_id=1, source_target_pairs={{1,0},{2,3},{5,4},{6,7},{9,8},{10,11},{13,12},{14,15},{17,16},{18,... | collective-permute-start | bytes 786440 | tf_op jit(solution)/shard_map/ppermute | solution.py:21
  22.8 19.6 %collective-permute-start.9 = (bf16[2,2,32,256]{3,2,1,0:T(8,128)(2,1)S(1)}, bf16[2,2,32,256]{3,2,1,0:T(8,128)(2,1)S(1)}, u32[]{:S(2)}, u32[]{:S(2)}) collective-permute-start(bf16[2,2,32,256]{3,2,1,0:T(8,128)(2,1)S(1)} %slice_select_fusion), channel_id=1, source_target_pairs={{0,10},{3,9},{4,14},{7,13},{8,18},{11,17},{12,22},{15,21},{16,26},... | collective-permute-start | bytes 196616 | tf_op jit(solution)/shard_map/ppermute | solution.py:21
  24.1 27.2 %collective-permute-start.6 = (bf16[1,8,32,256]{3,2,1,0:T(8,128)(2,1)S(1)}, bf16[1,8,32,256]{3,2,1,0:T(8,128)(2,1)S(1)}, u32[]{:S(2)}, u32[]{:S(2)}) collective-permute-start(bf16[1,8,32,256]{3,2,1,0:T(8,128)(2,1)S(1)} %collective-permute-done.3.p3), channel_id=1, source_target_pairs={{1,0},{2,3},{5,4},{6,7},{9,8},{10,11},{13,12},{14,15},{17,16},{18,... | collective-permute-start | bytes 393224 | tf_op jit(solution)/shard_map/ppermute | solution.py:21
  30.0 11.0 %collective-permute-start.10 = (bf16[1,2,32,256]{3,2,1,0:T(8,128)(2,1)S(1)}, bf16[1,2,32,256]{3,2,1,0:T(8,128)(2,1)S(1)}, u32[]{:S(2)}, u32[]{:S(2)}) collective-permute-start(bf16[1,2,32,256]{3,2,1,0:T(8,128)(2,1)S(1)} %slice.20), channel_id=1, source_target_pairs={{0,14},{3,13},{4,18},{7,17},{8,22},{11,21},{12,26},{15,25},{16,30}... | collective-permute-start | bytes 98312 | tf_op jit(solution)/shard_map/ppermute | solution.py:21
  41.0 9.2 %collective-permute-start.8 = (bf16[2,2,32,256]{3,2,1,0:T(8,128)(2,1)S(1)}, bf16[2,2,32,256]{3,2,1,0:T(8,128)(2,1)S(1)}, u32[]{:S(2)}, u32[]{:S(2)}) collective-permute-start(bf16[2,2,32,256]{3,2,1,0:T(8,128)(2,1)S(1)} %slice_select_fusion), channel_id=1, source_target_pairs={{0,6},{3,5},{4,10},{7,9},{8,14},{11,13},{12,18},{15,17},{16,22},{1... | collective-permute-start | bytes 196616 | tf_op jit(solution)/shard_map/ppermute | solution.py:21
  42.3 8.9 %collective-permute-start.7 = (bf16[2,2,32,256]{3,2,1,0:T(8,128)(2,1)S(1)}, bf16[2,2,32,256]{3,2,1,0:T(8,128)(2,1)S(1)}, u32[]{:S(2)}, u32[]{:S(2)}) collective-permute-start(bf16[2,2,32,256]{3,2,1,0:T(8,128)(2,1)S(1)} %slice_select_fusion), channel_id=1, source_target_pairs={{0,2},{3,1},{4,6},{7,5},{8,10},{11,9},{12,14},{15,13},{16,18},{19,... | collective-permute-start | bytes 196616 | tf_op jit(solution)/shard_map/ppermute | solution.py:21
  51.3 2.0 %copy-start = (bf16[3,3,3,256,256]{4,3,2,1,0:T(8,128)(2,1)S(1)}, bf16[3,3,3,256,256]{4,3,2,1,0:T(8,128)(2,1)}, u32[]{:S(2)}) copy-start(bf16[3,3,3,256,256]{4,3,2,1,0:T(8,128)(2,1)} %param.8) | copy-start | bytes 10616836
  53.3 0.9 %copy-start.1 = (bf16[1,2,4,32,256]{4,3,2,1,0:T(8,128)(2,1)S(1)}, bf16[1,2,4,32,256]{4,3,2,1,0:T(8,128)(2,1)}, u32[]{:S(2)}) copy-start(bf16[1,2,4,32,256]{4,3,2,1,0:T(8,128)(2,1)} %param.6) | copy-start | bytes 393220
  54.2 1.0 %copy-start.2 = (bf16[3,256,256]{2,1,0:T(8,128)(2,1)S(1)}, bf16[3,256,256]{2,1,0:T(8,128)(2,1)}, u32[]{:S(2)}) copy-start(bf16[3,256,256]{2,1,0:T(8,128)(2,1)} %upsample.1) | copy-start | bytes 1179652
  55.2 0.7 copy-start.3
  55.9 0.7 copy-start.4
